TPU v7x, 256 devices: a whole 4x4x8 slice. The times are simulated.
256 devices in a mesh: song: 4 (over y), seq: 64 (over z, x, core).
Axes of the slice: x: 4, y: 4, z: 8, core: 2. Of those that a mesh axis runs over, the one named last changes fastest.
Arguments:
- queries: bfloat16 [4, 8192, 2048], P('song', 'seq'), may hold values from -64 to 64
- keys: bfloat16 [4, 8192, 2048], P('song', 'seq'), may hold values from -64 to 64
- values: bfloat16 [4, 8192, 2048], P('song', 'seq'), may hold values from -6 to 6
- lyric_keys: bfloat16 [4, 384, 2048], P('song', 'seq'), may hold values from -64 to 64
- lyric_values: bfloat16 [4, 384, 2048], P('song', 'seq'), may hold values from -6 to 6
- q_gain: float32 [128], replicated, may hold values from 0.5 to 1.5
- k_gain: float32 [128], replicated, may hold values from 0.5 to 1.5
- cotangent: bfloat16 [4, 8192, 2048], P('song', 'seq'), may hold values from -12 to 12
- alignment: int32 [4, 64, 2], P('song', 'seq'), may hold values from -1 to 2, as said below
- lyric_len: int32 [4], P('song'), may hold values from 192 to 384
Outputs:
- attn_out: bfloat16 [4, 8192, 2048], P('song', 'seq')
- grad_queries: bfloat16 [4, 8192, 2048], P('song', 'seq')
- grad_keys: bfloat16 [4, 8192, 2048], P('song', 'seq')
- grad_values: bfloat16 [4, 8192, 2048], P('song', 'seq')
- grad_lyric_keys: bfloat16 [4, 384, 2048], P('song', 'seq')
- grad_lyric_values: bfloat16 [4, 384, 2048], P('song', 'seq')
- grad_q_gain: float32 [128], replicated
- grad_k_gain: float32 [128], replicated
Inputs may be any that keep to these rules, and one draw needn't show every extreme that they name: `alignment`: in each row the entries that are not -1 are distinct.
All inputs are finite; a program needn't handle non-finite values.
Results may differ from a plain program's by a relative error of at most 0.01.
Values may be sent and summed in bfloat16 or wider, within the bound.
A program may use at most 128 MiB of HBM per device.

v0:
```python
import functools

import jax
import jax.numpy as jnp
from jax import lax
from jax.sharding import PartitionSpec as P
from jax.experimental import pallas as pl
from jax.experimental.pallas import tpu as pltpu

BLK = 128
WIN = 1
TILES = 2


NORM_EPS = 1e-06


def extended_2(block, sides, width):
    for axis, dim in sides:
        count = lax.axis_size(axis)
        forward = [(i, i + 1) for i in range(count - 1)]
        backward = [(target, source) for source, target in forward]
        low = lax.ppermute(
            lax.slice_in_dim(block, block.shape[dim] - width, None, axis=dim), axis, forward
        )
        high = lax.ppermute(lax.slice_in_dim(block, 0, width, axis=dim), axis, backward)
        block = jnp.concatenate([low, block, high], axis=dim)
    return block


def seq_masks(count):
    masks = []
    m = 1
    while m < count:
        masks.append(m)
        m *= 2
    return masks


def swap_with(x, axis, mask):
    count = lax.axis_size(axis)
    return lax.ppermute(x, axis, [(i, i ^ mask) for i in range(count)])


def flip_bit(h, mask):
    return h + mask - 2 * mask * ((h // mask) % 2)


def gather_kernel(masks, x_ref, out_ref, local_sem, send_sem, recv_sem):
    me = lax.axis_index("seq")
    song = lax.axis_index("song")
    mesh_ids = pl.DeviceIdType.MESH
    barrier = pltpu.get_barrier_semaphore()
    for m in masks:
        pl.semaphore_signal(barrier, inc=1, device_id=(song, flip_bit(me, m)), device_id_type=mesh_ids)
    pl.semaphore_wait(barrier, len(masks))
    own = pltpu.make_async_copy(x_ref, out_ref.at[me], local_sem.at[0])
    own.start()
    own.wait()
    held = [me]
    idx = 0
    for m in masks:
        partner = flip_bit(me, m)
        copies = []
        for h in held:
            c = pltpu.make_async_remote_copy(
                src_ref=out_ref.at[h],
                dst_ref=out_ref.at[h],
                send_sem=send_sem.at[idx],
                recv_sem=recv_sem.at[idx],
                device_id=(song, partner),
                device_id_type=mesh_ids,
            )
            c.start()
            copies.append(c)
            idx += 1
        for c in copies:
            c.wait()
        held = held + [flip_bit(h, m) for h in held]


def gather_chunks(x, count, masks):
    return pl.pallas_call(
        functools.partial(gather_kernel, masks),
        out_shape=jax.ShapeDtypeStruct((count,) + x.shape, x.dtype),
        in_specs=[pl.BlockSpec(memory_space=pl.ANY)],
        out_specs=pl.BlockSpec(memory_space=pl.ANY),
        scratch_shapes=[
            pltpu.SemaphoreType.DMA((1,)),
            pltpu.SemaphoreType.DMA((count - 1,)),
            pltpu.SemaphoreType.DMA((count - 1,)),
        ],
        compiler_params=pltpu.CompilerParams(collective_id=0, has_side_effects=True),
    )(x)


def scatter_halving(parts, axis, order, rider):
    idx = lax.axis_index(axis)
    steps = len(order)
    buf = parts.reshape(parts.shape[:1] + (2,) * steps + parts.shape[2:])
    held = sorted(order, reverse=True)
    for mask in order:
        a = held.index(mask) + 1
        high = ((idx & mask) != 0).astype(jnp.int32)
        keep = lax.dynamic_index_in_dim(buf, high, axis=a, keepdims=False)
        send = lax.dynamic_index_in_dim(buf, 1 - high, axis=a, keepdims=False)
        got, other = swap_with((send.astype(jnp.bfloat16), rider), axis, mask)
        buf = keep + got.astype(keep.dtype)
        rider = rider + other
        held.pop(a - 1)
    return buf, rider


def sum_doubling(x, axes):
    for axis in axes:
        for mask in seq_masks(lax.axis_size(axis)):
            x = x + swap_with(x, axis, mask)
    return x


def norm_heads(inputs, norm_gain):
    row_values = inputs.astype(jnp.float32).reshape(inputs.shape[0], -1, norm_gain.shape[0])
    inverse = lax.rsqrt(jnp.mean(row_values * row_values, axis=-1, keepdims=True) + NORM_EPS)
    return (row_values * inverse * norm_gain, inverse)


def norm_back(inputs, inverse, norm_gain, grad_out):
    row_values = inputs.astype(jnp.float32).reshape(grad_out.shape)
    scaled = grad_out * norm_gain
    grad_input = inverse * scaled - row_values * inverse * inverse * inverse * jnp.mean(
        scaled * row_values, axis=-1, keepdims=True
    )
    grad_gain = jnp.sum(grad_out * row_values * inverse, axis=(0, 1))
    return (grad_input.reshape(inputs.shape), grad_gain)


def block_pass(query_rows, key_rows, value_rows, keep_mask, grad_rows, score_scale):
    scores = (
        jnp.einsum("qhd,khd->hqk", query_rows, key_rows, preferred_element_type=jnp.float32)
        * score_scale
    )
    exp_scores = jnp.where(keep_mask[None, None, :], jnp.exp(scores), 0.0)
    totals = jnp.sum(exp_scores, axis=2)
    prob_full = exp_scores / totals[:, :, None]
    prob_low = prob_full.astype(jnp.bfloat16)
    block_output = jnp.einsum(
        "hqk,khd->qhd", prob_low, value_rows, preferred_element_type=jnp.float32
    ).astype(jnp.bfloat16)
    delta_rows = jnp.sum(grad_rows.astype(jnp.float32) * block_output.astype(jnp.float32), axis=2).T
    grad_prob = jnp.einsum(
        "qhd,khd->hqk", grad_rows, value_rows, preferred_element_type=jnp.float32
    )
    grad_score = (prob_full * (grad_prob - delta_rows[:, :, None])).astype(jnp.bfloat16)
    query_gradient = (
        jnp.einsum("hqk,khd->qhd", grad_score, key_rows, preferred_element_type=jnp.float32)
        * score_scale
    )
    grad_key = (
        jnp.einsum("hqk,qhd->khd", grad_score, query_rows, preferred_element_type=jnp.float32)
        * score_scale
    )
    value_gradient = jnp.einsum(
        "hqk,qhd->khd", prob_low, grad_rows, preferred_element_type=jnp.float32
    )
    return (block_output, query_gradient, grad_key, value_gradient)


def attention_kernel(
    tiles_ref, q_ref, ek_ref, ev_ref, lk0_ref, lk1_ref, lv0_ref, lv1_ref, g_ref, m_ref, qg_ref, kg_ref,
    o_ref, dqi_ref, dke_ref, dve_ref, part_ref, gain_ref, *, scale
):
    f32 = jnp.float32
    window = ek_ref.shape[0]
    q_gain = qg_ref[...]
    k_gain = kg_ref[...]

    def normed(x_ref, gain):
        x = x_ref[...].astype(f32)
        inv = lax.rsqrt(jnp.mean(x * x, axis=1, keepdims=True) + NORM_EPS)
        return x, inv, (x * inv * gain).astype(jnp.bfloat16)

    qx, qinv, q = normed(q_ref, q_gain)
    kx, kinv, kn = normed(ek_ref, k_gain)
    lx0, linv0, ln0 = normed(lk0_ref, k_gain)
    lx1, linv1, ln1 = normed(lk1_ref, k_gain)
    g = g_ref[...]
    k = jnp.concatenate([kn, ln0, ln1], axis=0)
    v = jnp.concatenate([ev_ref[...], lv0_ref[...], lv1_ref[...]], axis=0)
    keep = m_ref[...] > 0.0
    nt = (((1,), (1,)), ((), ()))
    tn = (((0,), (0,)), ((), ()))
    s = lax.dot_general(q, k, nt, preferred_element_type=f32) * scale
    e = jnp.where(keep, jnp.exp(s), 0.0)
    tot = jnp.sum(e, axis=1, keepdims=True)
    p = e / tot
    p_low = p.astype(jnp.bfloat16)
    o = jnp.dot(p_low, v, preferred_element_type=f32).astype(jnp.bfloat16)
    o_ref[...] = o
    delta = jnp.sum(g.astype(f32) * o.astype(f32), axis=1, keepdims=True)
    dp = lax.dot_general(g, v, nt, preferred_element_type=f32)
    ds = (p * (dp - delta)).astype(jnp.bfloat16)
    dq = jnp.dot(ds, k, preferred_element_type=f32) * scale
    dk = lax.dot_general(ds, q, tn, preferred_element_type=f32) * scale
    dv = lax.dot_general(p_low, g, tn, preferred_element_type=f32)
    scaled = dq * q_gain
    dqi_ref[...] = (
        qinv * scaled - qx * qinv * qinv * qinv * jnp.mean(scaled * qx, axis=1, keepdims=True)
    ).astype(jnp.bfloat16)
    dke_ref[...] = dk[:window]
    dve_ref[...] = dv[:window]
    for j in range(part_ref.shape[1] // BLK):
        for c, d in enumerate((dk, dv)):
            placed = jnp.zeros((BLK, d.shape[1]), f32)
            for s in range(tiles_ref.shape[0]):
                rows = d[window + s * BLK : window + (s + 1) * BLK]
                placed = placed + jnp.where(tiles_ref[s] == j, rows, 0.0)
            part_ref[c, j * BLK : (j + 1) * BLK, :] = placed
    gq = jnp.sum(dq * qx * qinv, axis=0, keepdims=True)
    gk = (
        jnp.sum(dk[:window] * kx * kinv, axis=0, keepdims=True)
        + jnp.sum(dk[window : window + BLK] * lx0 * linv0, axis=0, keepdims=True)
        + jnp.sum(dk[window + BLK :] * lx1 * linv1, axis=0, keepdims=True)
    )
    gain_ref[...] = jnp.concatenate([gq, gk, jnp.zeros((6, gq.shape[1]), f32)], axis=0)


def attention_block(tiles, q, ek, ev, lk, lv, g, keep, q_gain, k_gain, scale):
    lyric_rows = lk.shape[0]
    rows, width = q.shape
    head_size = q_gain.shape[0]
    window = ek.shape[0]
    slots = tiles.shape[0]
    heads = width // head_size
    f32 = jnp.float32

    def col(r):
        return pl.BlockSpec((r, head_size), lambda h, t: (0, h))

    def slot(s):
        return pl.BlockSpec((BLK, head_size), lambda h, t: (jnp.maximum(t[s], 0), h))

    whole = pl.BlockSpec((1, head_size), lambda h, t: (0, 0))
    grid_spec = pltpu.PrefetchScalarGridSpec(
        num_scalar_prefetch=1,
        grid=(heads,),
        in_specs=[col(rows), col(window), col(window), slot(0), slot(1), slot(0), slot(1), col(rows),
                  pl.BlockSpec((1, keep.shape[1]), lambda h, t: (0, 0)), whole, whole],
        out_specs=[col(rows), col(rows), col(window), col(window),
                   pl.BlockSpec((2, lyric_rows, head_size), lambda h, t: (0, 0, h)), col(8)],
    )
    return pl.pallas_call(
        lambda *refs: attention_kernel(*refs, scale=scale),
        grid_spec=grid_spec,
        out_shape=[
            jax.ShapeDtypeStruct((rows, width), jnp.bfloat16),
            jax.ShapeDtypeStruct((rows, width), jnp.bfloat16),
            jax.ShapeDtypeStruct((window, width), f32),
            jax.ShapeDtypeStruct((window, width), f32),
            jax.ShapeDtypeStruct((2, lyric_rows, width), f32),
            jax.ShapeDtypeStruct((8, width), f32),
        ],
    )(tiles, q, ek, ev, lk, lk, lv, lv, g, keep, q_gain.reshape(1, head_size), k_gain.reshape(1, head_size))


def body(
    queries, keys, values, lyric_keys, lyric_values, q_gain, k_gain, cotangent, alignment, lyric_len
):
    head_size = q_gain.shape[0]
    model_width = queries.shape[2]
    head_count = model_width // head_size
    frames = queries.shape[1]
    lyric_local = lyric_keys.shape[1]
    seq_count = lax.axis_size("seq")
    border_rows = WIN * BLK
    window_extent = (2 * WIN + 1) * BLK
    score_scale = head_size ** (-0.5)
    total_frames = frames * seq_count
    first_frame = lax.axis_index("seq") * frames
    lyric_total = lyric_local * seq_count
    lyric_blocks = lyric_total // BLK
    masks = seq_masks(seq_count)

    lyric_pair = jnp.stack([lyric_keys[0], lyric_values[0]])
    lyric_all = gather_chunks(lyric_pair, seq_count, masks[::-1])
    lyric_all = jnp.swapaxes(lyric_all, 0, 1).reshape(2, lyric_total, model_width)

    query_raw = queries[0]
    lyric_inv = norm_heads(lyric_keys[0], k_gain)[1]

    stacked = jnp.stack([keys[0], values[0]])
    extended = extended_2(stacked, (("seq", 1),), border_rows)
    key_raw = keys[0]
    key_inv = norm_heads(key_raw, k_gain)[1]
    length = lyric_len[0]

    position = first_frame - border_rows + jnp.arange(window_extent, dtype=jnp.int32)
    audio_mask = (position >= 0) & (position < total_frames)
    tile_ids = alignment[0, 0]
    tiles = jnp.maximum(tile_ids, 0)
    lyric_mask = jnp.concatenate(
        [(tile_ids[s] >= 0) & (tiles[s] * BLK + jnp.arange(BLK, dtype=jnp.int32) < length) for s in range(TILES)]
    )
    keep_mask = jnp.concatenate([audio_mask, lyric_mask], axis=0).astype(jnp.float32)[None]
    block_output, unnormed_query_gradient, ext_grad_key, ext_grad_val, parts, gain_rows = attention_block(
        tile_ids,
        query_raw,
        extended[0],
        extended[1],
        lyric_all[0],
        lyric_all[1],
        cotangent[0],
        keep_mask,
        q_gain,
        k_gain,
        score_scale,
    )
    ext_grad_key = ext_grad_key.reshape(window_extent, head_count, head_size)
    ext_grad_val = ext_grad_val.reshape(window_extent, head_count, head_size)
    gains = jnp.sum(gain_rows[:2].reshape(2, head_count, head_size), axis=1)
    summed, gains = scatter_halving(parts.reshape(2, seq_count, lyric_local, model_width), "seq", masks, gains)
    total_gains = sum_doubling(gains, ("song",))
    summed_key = summed[0].reshape(lyric_local, head_count, head_size)
    summed_val = summed[1]

    own_grad_key = ext_grad_key[border_rows : border_rows + frames]
    own_grad_val = ext_grad_val[border_rows : border_rows + frames]
    rims = jnp.stack(
        [
            jnp.concatenate(
                [ext_grad_key[:border_rows], ext_grad_key[border_rows + frames :]], axis=0
            ).reshape(2 * border_rows, model_width),
            jnp.concatenate(
                [ext_grad_val[:border_rows], ext_grad_val[border_rows + frames :]], axis=0
            ).reshape(2 * border_rows, model_width),
        ]
    )
    received = extended_2(rims.astype(jnp.bfloat16), (("seq", 1),), border_rows).astype(rims.dtype)
    from_left = received[:, :border_rows].reshape(2, border_rows, head_count, head_size)
    from_right = received[:, 3 * border_rows :].reshape(2, border_rows, head_count, head_size)
    own_grad_key = (
        own_grad_key.at[:border_rows]
        .add(from_left[0])
        .at[frames - border_rows :]
        .add(from_right[0])
    )
    own_grad_val = (
        own_grad_val.at[:border_rows]
        .add(from_left[1])
        .at[frames - border_rows :]
        .add(from_right[1])
    )
    unnormed_key_gradient = norm_back(key_raw, key_inv, k_gain, own_grad_key)[0]
    unnormed_lyric_gradient = norm_back(lyric_keys[0], lyric_inv, k_gain, summed_key)[0]
    return (
        block_output.reshape(1, frames, model_width),
        unnormed_query_gradient[None],
        unnormed_key_gradient.astype(jnp.bfloat16)[None],
        own_grad_val.reshape(1, frames, model_width).astype(jnp.bfloat16),
        unnormed_lyric_gradient.astype(jnp.bfloat16)[None],
        summed_val.astype(jnp.bfloat16)[None],
        total_gains[0],
        total_gains[1],
    )


def solution(mesh):
    in_specs = (
        P("song", "seq", None),
        P("song", "seq", None),
        P("song", "seq", None),
        P("song", "seq", None),
        P("song", "seq", None),
        P(),
        P(),
        P("song", "seq", None),
        P("song", "seq", None),
        P("song"),
    )
    out_specs = (
        P("song", "seq", None),
        P("song", "seq", None),
        P("song", "seq", None),
        P("song", "seq", None),
        P("song", "seq", None),
        P("song", "seq", None),
        P(),
        P(),
    )
    return jax.shard_map(body, mesh=mesh, in_specs=in_specs, out_specs=out_specs, check_vma=False)
```

profile of v0, /device:TPU:16, one launch (start us, length us, event | category | flops | bytes accessed | tf_op | source)
XLA Modules:
  0.0 229.7 jit_solution(11600947341171134552)
XLA Ops:
  0.7 2.2 convert_bitcast_fusion.5
  4.8 2.8 %collective-permute-start = (bf16[2,128,2048]{2,1,0:T(8,128)(2,1)}, bf16[2,128,2048]{2,1,0:T(8,128)(2,1)}, u32[]{:S(2)}, u32[]{:S(2)}) collective-permute-start(bf16[2,128,2048]{2,1,0:T(8,128)(2,1)} %constant_dynamic-update-slice_fusion), channel_id=1, source_target_pairs={{0,1},{1,2},{2,3},{3,4},{4,5},{5,6},{6,7},{7,8},{8,9},{9,10},{10,1... | collective-permute-start | bytes 3145736 | tf_op jit(solution)/shard_map/ppermute | solution.py:23
  10.1 74.6 %shard_map.181 = bf16[64,2,6,2048]{3,2,1,0:T(8,128)(2,1)} custom-call(bf16[2,6,2048]{2,1,0:T(8,128)(2,1)} %pad_maximum_fusion.7.x_ref), custom_call_target="tpu_custom_call" | custom-call | tf_op jit(solution)/shard_map/pallas_call | solution.py:83
  84.8 4.0 %fusion.24 = (bf16[1,64,6,2048]{3,2,0,1:T(8,128)(2,1)S(1)}, bf16[1,64,6,2048]{3,2,0,1:T(8,128)(2,1)}) fusion(bf16[2,64,6,2048]{3,2,0,1:T(8,128)(2,1)} %bitcast.158), kind=kLoop, calls=%fused_computation.86 | loop fusion | bytes 6291456 | tf_op jit(solution)/shard_map/slice | solution.py:310
  92.7 3.7 %squeeze.76.refs_4_.refs_5_ = bf16[384,2048]{1,0:T(8,128)(2,1)} reshape(bf16[1,64,6,2048]{3,2,0,1:T(8,128)(2,1)} %get-tuple-element.119) | data formatting | bytes 3145728 | tf_op jit(solution)/shard_map/squeeze | solution.py:309
  98.5 2.1 pad_maximum_fusion
  100.6 2.0 slice_bitcast_fusion
  102.6 20.4 %shard_map.182 = (bf16[128,2048]{1,0:T(8,128)(2,1)}, bf16[128,2048]{1,0:T(8,128)(2,1)}, f32[384,2048]{1,0:T(8,128)}, f32[384,2048]{1,0:T(8,128)}, f32[2,384,2048]{2,1,0:T(8,128)}, /*index=5*/f32[8,2048]{1,0:T(8,128)}) custom-call(s32[2]{0:T(128)} %bitcast.169, bf16[128,2048]{1,0:T(8,128)(2,1)} %bitcast.162, bf16[384,2048]{1,0:T(8,128)(2,1)} %get-tuple-element.121.refs_2_, ...), custom_call_target="tpu_custom_call" | custom-call | tf_op jit(solution)/shard_map/pallas_call | solution.py:251
  126.4 7.6 %copy.21 = f32[2,384,2048]{2,0,1:T(2,128)S(1)} copy(f32[2,384,2048]{2,1,0:T(8,128)} %get-tuple-element.98) | data formatting | bytes 12582912 | tf_op jit(solution)/shard_map/pallas_call | solution.py:251
  136.8 2.6 %collective-permute-done.12 = f32[2,128]{1,0:T(2,128)S(1)} collective-permute-done((f32[2,128]{1,0:T(2,128)S(1)}, f32[2,128]{1,0:T(2,128)S(1)}, u32[]{:S(2)}, u32[]{:S(2)}) %collective-permute-start.12) | collective-permute-done | bytes 1056 | tf_op jit(solution)/shard_map/ppermute | solution.py:42
  139.4 2.5 %collective-permute-start.13 = (f32[2,128]{1,0:T(2,128)S(1)}, f32[2,128]{1,0:T(2,128)S(1)}, u32[]{:S(2)}, u32[]{:S(2)}) collective-permute-start(f32[2,128]{1,0:T(2,128)S(1)} %add.235), channel_id=1, source_target_pairs={{0,8},{1,9},{2,10},{3,11},{4,12},{5,13},{6,14},{7,15},{8,0},{9,1},... | collective-permute-start | bytes 3080 | tf_op jit(solution)/shard_map/ppermute | solution.py:42
  144.9 3.0 %collective-permute-done.14 = f32[2,128]{1,0:T(2,128)S(1)} collective-permute-done((f32[2,128]{1,0:T(2,128)S(1)}, f32[2,128]{1,0:T(2,128)S(1)}, u32[]{:S(2)}, u32[]{:S(2)}) %collective-permute-start.14) | collective-permute-done | bytes 1056 | tf_op jit(solution)/shard_map/ppermute | solution.py:42
  147.9 3.3 %collective-permute-start.15 = (f32[2,128]{1,0:T(2,128)S(1)}, f32[2,128]{1,0:T(2,128)S(1)}, u32[]{:S(2)}, u32[]{:S(2)}) collective-permute-start(f32[2,128]{1,0:T(2,128)S(1)} %add.237), channel_id=1, source_target_pairs={{0,32},{1,33},{2,34},{3,35},{4,36},{5,37},{6,38},{7,39},{8,40},{9,... | collective-permute-start | bytes 3080 | tf_op jit(solution)/shard_map/ppermute | solution.py:42
  151.3 4.0 %collective-permute-done.15 = f32[2,128]{1,0:T(2,128)S(1)} collective-permute-done((f32[2,128]{1,0:T(2,128)S(1)}, f32[2,128]{1,0:T(2,128)S(1)}, u32[]{:S(2)}, u32[]{:S(2)}) %collective-permute-start.15) | collective-permute-done | bytes 1056 | tf_op jit(solution)/shard_map/ppermute | solution.py:42
  162.7 5.1 %collective-permute-start.5 = (bf16[2,2,2,2,2,6,2048]{6,0,5,4,3,2,1:T(2,128)(2,1)S(1)}, bf16[2,2,2,2,2,6,2048]{6,0,5,4,3,2,1:T(2,128)(2,1)S(1)}, u32[]{:S(2)}, u32[]{:S(2)}) collective-permute-start(bf16[2,2,2,2,2,6,2048]{6,0,5,4,3,2,1:T(2,128)(2,1)S(1)} %fusion.12), channel_id=1, source_target_pairs={{0,2},{1,3},{2,0},{3,1},{4,6},{5,7},{6,4},{7,5},{8,10},{9,11},{10,... | collective-permute-start | bytes 2359304 | tf_op jit(solution)/shard_map/ppermute | solution.py:42
  169.8 24.2 %collective-permute-done.5 = bf16[2,2,2,2,2,6,2048]{6,0,5,4,3,2,1:T(2,128)(2,1)S(1)} collective-permute-done((bf16[2,2,2,2,2,6,2048]{6,0,5,4,3,2,1:T(2,128)(2,1)S(1)}, bf16[2,2,2,2,2,6,2048]{6,0,5,4,3,2,1:T(2,128)(2,1)S(1)}, u32[]{:S(2)}, u32[]{:S(2)}) %collective-permute-start.5) | collective-permute-done | bytes 786464 | tf_op jit(solution)/shard_map/ppermute | solution.py:42
  197.2 7.6 %collective-permute-done.6 = bf16[2,2,2,2,6,2048]{5,0,4,3,2,1:T(2,128)(2,1)S(1)} collective-permute-done((bf16[2,2,2,2,6,2048]{5,0,4,3,2,1:T(2,128)(2,1)S(1)}, bf16[2,2,2,2,6,2048]{5,0,4,3,2,1:T(2,128)(2,1)S(1)}, u32[]{:S(2)}, u32[]{:S(2)}) %collective-permute-start.6) | collective-permute-done | bytes 393248 | tf_op jit(solution)/shard_map/ppermute | solution.py:42
  205.6 2.1 collective-permute-start.7
  207.7 4.3 %collective-permute-done.7 = bf16[2,2,2,6,2048]{4,0,3,2,1:T(2,128)(2,1)S(1)} collective-permute-done((bf16[2,2,2,6,2048]{4,0,3,2,1:T(2,128)(2,1)S(1)}, bf16[2,2,2,6,2048]{4,0,3,2,1:T(2,128)(2,1)S(1)}, u32[]{:S(2)}, u32[]{:S(2)}) %collective-permute-start.7) | collective-permute-done | bytes 196640 | tf_op jit(solution)/shard_map/ppermute | solution.py:42
  212.3 1.9 collective-permute-start.8
  214.8 2.1 fusion.15
  216.9 2.5 %collective-permute-done.8 = bf16[2,2,6,2048]{3,0,2,1:T(2,128)(2,1)S(1)} collective-permute-done((bf16[2,2,6,2048]{3,0,2,1:T(2,128)(2,1)S(1)}, bf16[2,2,6,2048]{3,0,2,1:T(2,128)(2,1)S(1)}, u32[]{:S(2)}, u32[]{:S(2)}) %collective-permute-start.8) | collective-permute-done | bytes 98336 | tf_op jit(solution)/shard_map/ppermute | solution.py:42
  219.6 3.1 %collective-permute-start.9 = (bf16[2,6,2048]{2,0,1:T(2,128)(2,1)S(1)}, bf16[2,6,2048]{2,0,1:T(2,128)(2,1)S(1)}, u32[]{:S(2)}, u32[]{:S(2)}) collective-permute-start(bf16[2,6,2048]{2,0,1:T(2,128)(2,1)S(1)} %fusion.20), channel_id=1, source_target_pairs={{0,32},{1,33},{2,34},{3,35},{4,36},{5,37},{6,38},{7,39},{8,40},{9,... | collective-permute-start | bytes 147464 | tf_op jit(solution)/shard_map/ppermute | solution.py:42
  223.7 4.2 %collective-permute-done.9 = bf16[2,6,2048]{2,0,1:T(2,128)(2,1)S(1)} collective-permute-done((bf16[2,6,2048]{2,0,1:T(2,128)(2,1)S(1)}, bf16[2,6,2048]{2,0,1:T(2,128)(2,1)S(1)}, u32[]{:S(2)}, u32[]{:S(2)}) %collective-permute-start.9) | collective-permute-done | bytes 49184 | tf_op jit(solution)/shard_map/ppermute | solution.py:42
  (103 shorter events, 33.5 us)
Async XLA Ops:
  0.6 8.3 %copy-start.8 = (s32[1,1,2]{2,1,0:T(1,128)S(1)}, s32[1,1,2]{2,1,0:T(1,128)}, u32[]{:S(2)}) copy-start(s32[1,1,2]{2,1,0:T(1,128)} %param.34) | copy-start | bytes 28
  0.6 8.8 %copy-start.4 = (bf16[1,6,2048]{2,1,0:T(8,128)(2,1)S(1)}, bf16[1,6,2048]{2,1,0:T(8,128)(2,1)}, u32[]{:S(2)}) copy-start(bf16[1,6,2048]{2,1,0:T(8,128)(2,1)} %param.29) | copy-start | bytes 73732
  0.7 8.8 %copy-start.5 = (bf16[1,6,2048]{2,1,0:T(8,128)(2,1)S(1)}, bf16[1,6,2048]{2,1,0:T(8,128)(2,1)}, u32[]{:S(2)}) copy-start(bf16[1,6,2048]{2,1,0:T(8,128)(2,1)} %param.30) | copy-start | bytes 73732
  4.8 93.7 %collective-permute-start = (bf16[2,128,2048]{2,1,0:T(8,128)(2,1)}, bf16[2,128,2048]{2,1,0:T(8,128)(2,1)}, u32[]{:S(2)}, u32[]{:S(2)}) collective-permute-start(bf16[2,128,2048]{2,1,0:T(8,128)(2,1)} %constant_dynamic-update-slice_fusion), channel_id=1, source_target_pairs={{0,1},{1,2},{2,3},{3,4},{4,5},{5,6},{6,7},{7,8},{8,9},{9,10},{10,1... | collective-permute-start | bytes 3145736 | tf_op jit(solution)/shard_map/ppermute | solution.py:23
  7.6 90.9 %collective-permute-start.1 = (bf16[2,128,2048]{2,1,0:T(8,128)(2,1)}, bf16[2,128,2048]{2,1,0:T(8,128)(2,1)}, u32[]{:S(2)}, u32[]{:S(2)}) collective-permute-start(bf16[2,128,2048]{2,1,0:T(8,128)(2,1)} %constant_dynamic-update-slice_fusion), channel_id=1, source_target_pairs={{1,0},{2,1},{3,2},{4,3},{5,4},{6,5},{7,6},{8,7},{9,8},{10,9},{11,1... | collective-permute-start | bytes 3145736 | tf_op jit(solution)/shard_map/ppermute | solution.py:26
  92.7 5.8 %copy-start.6 = (f32[128]{0:T(128)S(1)}, f32[128]{0:T(128)}, u32[]{:S(2)}) copy-start(f32[128]{0:T(128)} %param.32) | copy-start | bytes 1540
  123.9 1.3 collective-permute-start.10
  125.1 8.9 %collective-permute-start.11 = (f32[2,128]{1,0:T(2,128)S(1)}, f32[2,128]{1,0:T(2,128)S(1)}, u32[]{:S(2)}, u32[]{:S(2)}) collective-permute-start(f32[2,128]{1,0:T(2,128)S(1)} %add.233), channel_id=1, source_target_pairs={{0,2},{1,3},{2,0},{3,1},{4,6},{5,7},{6,4},{7,5},{8,10},{9,11},{10,... | collective-permute-start | bytes 3080 | tf_op jit(solution)/shard_map/ppermute | solution.py:42
  134.0 5.3 %collective-permute-start.12 = (f32[2,128]{1,0:T(2,128)S(1)}, f32[2,128]{1,0:T(2,128)S(1)}, u32[]{:S(2)}, u32[]{:S(2)}) collective-permute-start(f32[2,128]{1,0:T(2,128)S(1)} %add.234), channel_id=1, source_target_pairs={{0,4},{1,5},{2,6},{3,7},{4,0},{5,1},{6,2},{7,3},{8,12},{9,13},{10,... | collective-permute-start | bytes 3080 | tf_op jit(solution)/shard_map/ppermute | solution.py:42
  136.4 23.8 %collective-permute-start.4 = (bf16[2,2,2,2,2,2,6,2048]{7,0,6,5,4,3,2,1:T(2,128)(2,1)S(1)}, bf16[2,2,2,2,2,2,6,2048]{7,0,6,5,4,3,2,1:T(2,128)(2,1)S(1)}, u32[]{:S(2)}, u32[]{:S(2)}) collective-permute-start(bf16[2,2,2,2,2,2,6,2048]{7,0,6,5,4,3,2,1:T(2,128)(2,1)S(1)} %fusion), channel_id=1, source_target_pairs={{0,1},{1,0},{2,3},{3,2},{4,5},{5,4},{6,7},{7,6},{8,9},{9,8},{10,11... | collective-permute-start | bytes 4718600 | tf_op jit(solution)/shard_map/ppermute | solution.py:42
  139.4 4.0 %collective-permute-start.13 = (f32[2,128]{1,0:T(2,128)S(1)}, f32[2,128]{1,0:T(2,128)S(1)}, u32[]{:S(2)}, u32[]{:S(2)}) collective-permute-start(f32[2,128]{1,0:T(2,128)S(1)} %add.235), channel_id=1, source_target_pairs={{0,8},{1,9},{2,10},{3,11},{4,12},{5,13},{6,14},{7,15},{8,0},{9,1},... | collective-permute-start | bytes 3080 | tf_op jit(solution)/shard_map/ppermute | solution.py:42
  143.4 4.5 %collective-permute-start.14 = (f32[2,128]{1,0:T(2,128)S(1)}, f32[2,128]{1,0:T(2,128)S(1)}, u32[]{:S(2)}, u32[]{:S(2)}) collective-permute-start(f32[2,128]{1,0:T(2,128)S(1)} %add.236), channel_id=1, source_target_pairs={{0,16},{1,17},{2,18},{3,19},{4,20},{5,21},{6,22},{7,23},{8,24},{9,... | collective-permute-start | bytes 3080 | tf_op jit(solution)/shard_map/ppermute | solution.py:42
  147.9 7.5 %collective-permute-start.15 = (f32[2,128]{1,0:T(2,128)S(1)}, f32[2,128]{1,0:T(2,128)S(1)}, u32[]{:S(2)}, u32[]{:S(2)}) collective-permute-start(f32[2,128]{1,0:T(2,128)S(1)} %add.237), channel_id=1, source_target_pairs={{0,32},{1,33},{2,34},{3,35},{4,36},{5,37},{6,38},{7,39},{8,40},{9,... | collective-permute-start | bytes 3080 | tf_op jit(solution)/shard_map/ppermute | solution.py:42
  155.4 4.1 %collective-permute-start.16 = (f32[2,128]{1,0:T(2,128)S(1)}, f32[2,128]{1,0:T(2,128)S(1)}, u32[]{:S(2)}, u32[]{:S(2)}) collective-permute-start(f32[2,128]{1,0:T(2,128)S(1)} %add.238), channel_id=1, source_target_pairs={{0,64},{64,0},{128,192},{192,128},{1,65},{65,1},{129,193},{193,129... | collective-permute-start | bytes 3080 | tf_op jit(solution)/shard_map/ppermute | solution.py:42
  156.8 11.8 %collective-permute-start.2 = (bf16[2,128,2048]{2,1,0:T(8,128)(2,1)S(1)}, bf16[2,128,2048]{2,1,0:T(8,128)(2,1)S(1)}, u32[]{:S(2)}, u32[]{:S(2)}) collective-permute-start(bf16[2,128,2048]{2,1,0:T(8,128)(2,1)S(1)} %get-tuple-element.122), channel_id=1, source_target_pairs={{0,1},{1,2},{2,3},{3,4},{4,5},{5,6},{6,7},{7,8},{8,9},{9,10},{10,1... | collective-permute-start | bytes 3145736 | tf_op jit(solution)/shard_map/ppermute | solution.py:23
  158.2 10.4 %collective-permute-start.3 = (bf16[2,128,2048]{2,1,0:T(8,128)(2,1)S(1)}, bf16[2,128,2048]{2,1,0:T(8,128)(2,1)S(1)}, u32[]{:S(2)}, u32[]{:S(2)}) collective-permute-start(bf16[2,128,2048]{2,1,0:T(8,128)(2,1)S(1)} %get-tuple-element.123), channel_id=1, source_target_pairs={{1,0},{2,1},{3,2},{4,3},{5,4},{6,5},{7,6},{8,7},{9,8},{10,9},{11,1... | collective-permute-start | bytes 3145736 | tf_op jit(solution)/shard_map/ppermute | solution.py:26
  159.5 8.6 %collective-permute-start.17 = (f32[2,128]{1,0:T(2,128)S(1)}, f32[2,128]{1,0:T(2,128)S(1)}, u32[]{:S(2)}, u32[]{:S(2)}) collective-permute-start(f32[2,128]{1,0:T(2,128)S(1)} %add.239), channel_id=1, source_target_pairs={{0,128},{64,192},{128,0},{192,64},{1,129},{65,193},{129,1},{193,65... | collective-permute-start | bytes 3080 | tf_op jit(solution)/shard_map/ppermute | solution.py:42
  162.7 31.3 %collective-permute-start.5 = (bf16[2,2,2,2,2,6,2048]{6,0,5,4,3,2,1:T(2,128)(2,1)S(1)}, bf16[2,2,2,2,2,6,2048]{6,0,5,4,3,2,1:T(2,128)(2,1)S(1)}, u32[]{:S(2)}, u32[]{:S(2)}) collective-permute-start(bf16[2,2,2,2,2,6,2048]{6,0,5,4,3,2,1:T(2,128)(2,1)S(1)} %fusion.12), channel_id=1, source_target_pairs={{0,2},{1,3},{2,0},{3,1},{4,6},{5,7},{6,4},{7,5},{8,10},{9,11},{10,... | collective-permute-start | bytes 2359304 | tf_op jit(solution)/shard_map/ppermute | solution.py:42
  169.8 26.7 %copy-start.2 = (f32[16,8,16,128]{3,2,1,0:T(8,128)S(1)}, f32[16,8,16,128]{3,2,1,0:T(8,128)}, u32[]{:S(2)}) copy-start(f32[16,8,16,128]{3,2,1,0:T(8,128)} %copy.24) | copy-start | bytes 3145732
  195.2 9.6 %collective-permute-start.6 = (bf16[2,2,2,2,6,2048]{5,0,4,3,2,1:T(2,128)(2,1)S(1)}, bf16[2,2,2,2,6,2048]{5,0,4,3,2,1:T(2,128)(2,1)S(1)}, u32[]{:S(2)}, u32[]{:S(2)}) collective-permute-start(bf16[2,2,2,2,6,2048]{5,0,4,3,2,1:T(2,128)(2,1)S(1)} %fusion.16), channel_id=1, source_target_pairs={{0,4},{1,5},{2,6},{3,7},{4,0},{5,1},{6,2},{7,3},{8,12},{9,13},{10,... | collective-permute-start | bytes 1179656 | tf_op jit(solution)/shard_map/ppermute | solution.py:42
  197.2 17.7 %copy-start.3 = (bf16[1,128,2048]{2,1,0:T(8,128)(2,1)S(1)}, bf16[1,128,2048]{2,1,0:T(8,128)(2,1)}, u32[]{:S(2)}) copy-start(bf16[1,128,2048]{2,1,0:T(8,128)(2,1)} %param.27) | copy-start | bytes 1572868
  205.6 6.4 %collective-permute-start.7 = (bf16[2,2,2,6,2048]{4,0,3,2,1:T(2,128)(2,1)S(1)}, bf16[2,2,2,6,2048]{4,0,3,2,1:T(2,128)(2,1)S(1)}, u32[]{:S(2)}, u32[]{:S(2)}) collective-permute-start(bf16[2,2,2,6,2048]{4,0,3,2,1:T(2,128)(2,1)S(1)} %fusion.17), channel_id=1, source_target_pairs={{0,8},{1,9},{2,10},{3,11},{4,12},{5,13},{6,14},{7,15},{8,0},{9,1},... | collective-permute-start | bytes 589832 | tf_op jit(solution)/shard_map/ppermute | solution.py:42
  212.3 7.2 %collective-permute-start.8 = (bf16[2,2,6,2048]{3,0,2,1:T(2,128)(2,1)S(1)}, bf16[2,2,6,2048]{3,0,2,1:T(2,128)(2,1)S(1)}, u32[]{:S(2)}, u32[]{:S(2)}) collective-permute-start(bf16[2,2,6,2048]{3,0,2,1:T(2,128)(2,1)S(1)} %fusion.18), channel_id=1, source_target_pairs={{0,16},{1,17},{2,18},{3,19},{4,20},{5,21},{6,22},{7,23},{8,24},{9,... | collective-permute-start | bytes 294920 | tf_op jit(solution)/shard_map/ppermute | solution.py:42
  219.6 8.2 %collective-permute-start.9 = (bf16[2,6,2048]{2,0,1:T(2,128)(2,1)S(1)}, bf16[2,6,2048]{2,0,1:T(2,128)(2,1)S(1)}, u32[]{:S(2)}, u32[]{:S(2)}) collective-permute-start(bf16[2,6,2048]{2,0,1:T(2,128)(2,1)S(1)} %fusion.20), channel_id=1, source_target_pairs={{0,32},{1,33},{2,34},{3,35},{4,36},{5,37},{6,38},{7,39},{8,40},{9,... | collective-permute-start | bytes 147464 | tf_op jit(solution)/shard_map/ppermute | solution.py:42
  (3 other events, 8.6 us)
where the time goes:
time: 231 us; the launch traced here: 230 us
  Pallas kernels  95.1 us (41%)
  waiting for transfers between devices  54.3 us (24%)
  starting transfers between devices  30.9 us (13%)
  local copies, waits for them, and re-layouts  30.7 us (13%)
  other arithmetic  14.4 us (6%)
  between operations  4.34 us (2%)
    pallas_call x1, Pallas kernels, gather_chunks(): pl.pallas_call(functools.partial(gather_kernel, masks), out_shape=jax.Sha...  74.6 us
    ppermute x14, waiting for transfers between devices, swap_with(): return lax.ppermute(x, axis, [(i, i ^ mask) for i in range(count)])  54.3 us
    ppermute x14, starting transfers between devices, swap_with(): return lax.ppermute(x, axis, [(i, i ^ mask) for i in range(count)])  24.1 us
    pallas_call x1, Pallas kernels, attention_block(): pl.pallas_call(lambda *refs: attention_kernel(*refs, scale=scale), grid_s...  20.4 us
    pallas_call x1, local copies, waits for them, and re-layouts, attention_block(): pl.pallas_call(lambda *refs: attention_kernel(*refs, scale=scale), grid_s...  7.64 us
  transfers between devices with their start and end apart: 18, of which 10 were waited for; matrix products, arithmetic and copies ran while one was open for 14% of the time, Pallas kernels for 32%

commit v1 on v0

--- a/solution.py
+++ b/solution.py
@@ -49,34 +49,29 @@
 def gather_kernel(masks, x_ref, out_ref, local_sem, send_sem, recv_sem):
     me = lax.axis_index("seq")
     song = lax.axis_index("song")
+    steps = len(masks)
+    slot = sum(((me // m) % 2) * (2 ** k) for k, m in enumerate(masks))
     mesh_ids = pl.DeviceIdType.MESH
     barrier = pltpu.get_barrier_semaphore()
     for m in masks:
         pl.semaphore_signal(barrier, inc=1, device_id=(song, flip_bit(me, m)), device_id_type=mesh_ids)
-    pl.semaphore_wait(barrier, len(masks))
-    own = pltpu.make_async_copy(x_ref, out_ref.at[me], local_sem.at[0])
+    pl.semaphore_wait(barrier, steps)
+    own = pltpu.make_async_copy(x_ref, out_ref.at[slot], local_sem.at[0])
     own.start()
     own.wait()
-    held = [me]
-    idx = 0
-    for m in masks:
-        partner = flip_bit(me, m)
-        copies = []
-        for h in held:
-            c = pltpu.make_async_remote_copy(
-                src_ref=out_ref.at[h],
-                dst_ref=out_ref.at[h],
-                send_sem=send_sem.at[idx],
-                recv_sem=recv_sem.at[idx],
-                device_id=(song, partner),
-                device_id_type=mesh_ids,
-            )
-            c.start()
-            copies.append(c)
-            idx += 1
-        for c in copies:
-            c.wait()
-        held = held + [flip_bit(h, m) for h in held]
+    for k, m in enumerate(masks):
+        size = 2 ** k
+        base = (slot // size) * size
+        c = pltpu.make_async_remote_copy(
+            src_ref=out_ref.at[pl.ds(base, size)],
+            dst_ref=out_ref.at[pl.ds(base, size)],
+            send_sem=send_sem.at[k],
+            recv_sem=recv_sem.at[k],
+            device_id=(song, flip_bit(me, m)),
+            device_id_type=mesh_ids,
+        )
+        c.start()
+        c.wait()
 
 
 def gather_chunks(x, count, masks):
@@ -87,8 +82,8 @@
         out_specs=pl.BlockSpec(memory_space=pl.ANY),
         scratch_shapes=[
             pltpu.SemaphoreType.DMA((1,)),
-            pltpu.SemaphoreType.DMA((count - 1,)),
-            pltpu.SemaphoreType.DMA((count - 1,)),
+            pltpu.SemaphoreType.DMA((len(masks),)),
+            pltpu.SemaphoreType.DMA((len(masks),)),
         ],
         compiler_params=pltpu.CompilerParams(collective_id=0, has_side_effects=True),
     )(x)
@@ -281,8 +276,11 @@
     masks = seq_masks(seq_count)
 
     lyric_pair = jnp.stack([lyric_keys[0], lyric_values[0]])
+    steps = len(masks)
     lyric_all = gather_chunks(lyric_pair, seq_count, masks[::-1])
-    lyric_all = jnp.swapaxes(lyric_all, 0, 1).reshape(2, lyric_total, model_width)
+    lyric_all = lyric_all.reshape((2,) * steps + lyric_pair.shape)
+    lyric_all = jnp.transpose(lyric_all, (steps,) + tuple(range(steps))[::-1] + (steps + 1, steps + 2))
+    lyric_all = lyric_all.reshape(2, lyric_total, model_width)
 
     query_raw = queries[0]
     lyric_inv = norm_heads(lyric_keys[0], k_gain)[1]

time: 231 us -> 230 us (level)
    reshape x0 -> x1, local copies, waits for them, and re-layouts: none -> 2.5 us  [body(): lyric_all = lyric_all.reshape((2,) * steps + lyric_pair.shape)]
    slice x1, local copies, waits for them, and re-layouts: 4.04 us -> 1.64 us  [body(): lyric_all[1]]
where the time goes in v1:
time: 230 us; the launch traced here: 229 us
  Pallas kernels  94.1 us (41%)
  waiting for transfers between devices  54.4 us (24%)
  local copies, waits for them, and re-layouts  30.8 us (13%)
  starting transfers between devices  30.5 us (13%)
  other arithmetic  14.4 us (6%)
  between operations  4.35 us (2%)
    pallas_call x1, Pallas kernels, gather_chunks(): pl.pallas_call(functools.partial(gather_kernel, masks), out_shape=jax.Sha...  73.7 us
    ppermute x14, waiting for transfers between devices, swap_with(): return lax.ppermute(x, axis, [(i, i ^ mask) for i in range(count)])  54.4 us
    ppermute x14, starting transfers between devices, swap_with(): return lax.ppermute(x, axis, [(i, i ^ mask) for i in range(count)])  23.9 us
    pallas_call x1, Pallas kernels, attention_block(): pl.pallas_call(lambda *refs: attention_kernel(*refs, scale=scale), grid_s...  20.4 us
    pallas_call x1, local copies, waits for them, and re-layouts, attention_block(): pl.pallas_call(lambda *refs: attention_kernel(*refs, scale=scale), grid_s...  7.64 us
  transfers between devices with their start and end apart: 18, of which 10 were waited for; matrix products, arithmetic and copies ran while one was open for 14% of the time, Pallas kernels for 32%

profile of v1, /device:TPU:16, one launch (start us, length us, event | category | flops | bytes accessed | tf_op | source)
XLA Modules:
  0.0 228.6 jit_solution(5803246178505937145)
XLA Ops:
  0.7 2.2 convert_bitcast_fusion.5
  4.7 2.7 %collective-permute-start = (bf16[2,128,2048]{2,1,0:T(8,128)(2,1)}, bf16[2,128,2048]{2,1,0:T(8,128)(2,1)}, u32[]{:S(2)}, u32[]{:S(2)}) collective-permute-start(bf16[2,128,2048]{2,1,0:T(8,128)(2,1)} %constant_dynamic-update-slice_fusion), channel_id=1, source_target_pairs={{0,1},{1,2},{2,3},{3,4},{4,5},{5,6},{6,7},{7,8},{8,9},{9,10},{10,1... | collective-permute-start | bytes 3145736 | tf_op jit(solution)/shard_map/ppermute | solution.py:23
  10.0 73.7 %shard_map.181 = bf16[64,2,6,2048]{3,2,1,0:T(8,128)(2,1)} custom-call(bf16[2,6,2048]{2,1,0:T(8,128)(2,1)} %pad_maximum_fusion.7.x_ref), custom_call_target="tpu_custom_call" | custom-call | tf_op jit(solution)/shard_map/pallas_call | solution.py:78
  83.7 2.5 %copy.44 = bf16[2,2,2,2,2,2,2,6,2048]{8,7,0,1,2,3,4,5,6:T(8,128)(2,1)S(1)} copy(bf16[2,2,2,2,2,2,2,6,2048]{8,7,6,5,4,3,2,1,0:T(8,128)(2,1)} %bitcast.158) | data formatting | bytes 6291456 | tf_op jit(solution)/shard_map/reshape | solution.py:281
  91.7 3.7 %squeeze.76.refs_4_.refs_5_ = bf16[384,2048]{1,0:T(8,128)(2,1)} reshape(bf16[1,2,2,2,2,2,2,6,2048]{8,7,6,5,4,3,2,1,0:T(8,128)(2,1)} %get-tuple-element.119) | data formatting | bytes 3145728 | tf_op jit(solution)/shard_map/squeeze | solution.py:307
  97.5 2.1 pad_maximum_fusion
  99.6 2.0 slice_bitcast_fusion
  101.6 20.4 %shard_map.182 = (bf16[128,2048]{1,0:T(8,128)(2,1)}, bf16[128,2048]{1,0:T(8,128)(2,1)}, f32[384,2048]{1,0:T(8,128)}, f32[384,2048]{1,0:T(8,128)}, f32[2,384,2048]{2,1,0:T(8,128)}, /*index=5*/f32[8,2048]{1,0:T(8,128)}) custom-call(s32[2]{0:T(128)} %bitcast.169, bf16[128,2048]{1,0:T(8,128)(2,1)} %bitcast.162, bf16[384,2048]{1,0:T(8,128)(2,1)} %get-tuple-element.121.refs_2_, ...), custom_call_target="tpu_custom_call" | custom-call | tf_op jit(solution)/shard_map/pallas_call | solution.py:246
  125.4 7.6 %copy.23 = f32[2,384,2048]{2,0,1:T(2,128)S(1)} copy(f32[2,384,2048]{2,1,0:T(8,128)} %get-tuple-element.98) | data formatting | bytes 12582912 | tf_op jit(solution)/shard_map/pallas_call | solution.py:246
  135.8 2.6 %collective-permute-done.12 = f32[2,128]{1,0:T(2,128)S(1)} collective-permute-done((f32[2,128]{1,0:T(2,128)S(1)}, f32[2,128]{1,0:T(2,128)S(1)}, u32[]{:S(2)}, u32[]{:S(2)}) %collective-permute-start.12) | collective-permute-done | bytes 1056 | tf_op jit(solution)/shard_map/ppermute | solution.py:42
  138.4 2.5 %collective-permute-start.13 = (f32[2,128]{1,0:T(2,128)S(1)}, f32[2,128]{1,0:T(2,128)S(1)}, u32[]{:S(2)}, u32[]{:S(2)}) collective-permute-start(f32[2,128]{1,0:T(2,128)S(1)} %add.235), channel_id=1, source_target_pairs={{0,8},{1,9},{2,10},{3,11},{4,12},{5,13},{6,14},{7,15},{8,0},{9,1},... | collective-permute-start | bytes 3080 | tf_op jit(solution)/shard_map/ppermute | solution.py:42
  143.9 3.0 %collective-permute-done.14 = f32[2,128]{1,0:T(2,128)S(1)} collective-permute-done((f32[2,128]{1,0:T(2,128)S(1)}, f32[2,128]{1,0:T(2,128)S(1)}, u32[]{:S(2)}, u32[]{:S(2)}) %collective-permute-start.14) | collective-permute-done | bytes 1056 | tf_op jit(solution)/shard_map/ppermute | solution.py:42
  146.9 3.2 %collective-permute-start.15 = (f32[2,128]{1,0:T(2,128)S(1)}, f32[2,128]{1,0:T(2,128)S(1)}, u32[]{:S(2)}, u32[]{:S(2)}) collective-permute-start(f32[2,128]{1,0:T(2,128)S(1)} %add.237), channel_id=1, source_target_pairs={{0,32},{1,33},{2,34},{3,35},{4,36},{5,37},{6,38},{7,39},{8,40},{9,... | collective-permute-start | bytes 3080 | tf_op jit(solution)/shard_map/ppermute | solution.py:42
  150.3 4.1 %collective-permute-done.15 = f32[2,128]{1,0:T(2,128)S(1)} collective-permute-done((f32[2,128]{1,0:T(2,128)S(1)}, f32[2,128]{1,0:T(2,128)S(1)}, u32[]{:S(2)}, u32[]{:S(2)}) %collective-permute-start.15) | collective-permute-done | bytes 1056 | tf_op jit(solution)/shard_map/ppermute | solution.py:42
  161.7 5.1 %collective-permute-start.5 = (bf16[2,2,2,2,2,6,2048]{6,0,5,4,3,2,1:T(2,128)(2,1)S(1)}, bf16[2,2,2,2,2,6,2048]{6,0,5,4,3,2,1:T(2,128)(2,1)S(1)}, u32[]{:S(2)}, u32[]{:S(2)}) collective-permute-start(bf16[2,2,2,2,2,6,2048]{6,0,5,4,3,2,1:T(2,128)(2,1)S(1)} %fusion.12), channel_id=1, source_target_pairs={{0,2},{1,3},{2,0},{3,1},{4,6},{5,7},{6,4},{7,5},{8,10},{9,11},{10,... | collective-permute-start | bytes 2359304 | tf_op jit(solution)/shard_map/ppermute | solution.py:42
  168.9 24.2 %collective-permute-done.5 = bf16[2,2,2,2,2,6,2048]{6,0,5,4,3,2,1:T(2,128)(2,1)S(1)} collective-permute-done((bf16[2,2,2,2,2,6,2048]{6,0,5,4,3,2,1:T(2,128)(2,1)S(1)}, bf16[2,2,2,2,2,6,2048]{6,0,5,4,3,2,1:T(2,128)(2,1)S(1)}, u32[]{:S(2)}, u32[]{:S(2)}) %collective-permute-start.5) | collective-permute-done | bytes 786464 | tf_op jit(solution)/shard_map/ppermute | solution.py:42
  196.2 7.6 %collective-permute-done.6 = bf16[2,2,2,2,6,2048]{5,0,4,3,2,1:T(2,128)(2,1)S(1)} collective-permute-done((bf16[2,2,2,2,6,2048]{5,0,4,3,2,1:T(2,128)(2,1)S(1)}, bf16[2,2,2,2,6,2048]{5,0,4,3,2,1:T(2,128)(2,1)S(1)}, u32[]{:S(2)}, u32[]{:S(2)}) %collective-permute-start.6) | collective-permute-done | bytes 393248 | tf_op jit(solution)/shard_map/ppermute | solution.py:42
  204.6 2.1 collective-permute-start.7
  206.7 4.3 %collective-permute-done.7 = bf16[2,2,2,6,2048]{4,0,3,2,1:T(2,128)(2,1)S(1)} collective-permute-done((bf16[2,2,2,6,2048]{4,0,3,2,1:T(2,128)(2,1)S(1)}, bf16[2,2,2,6,2048]{4,0,3,2,1:T(2,128)(2,1)S(1)}, u32[]{:S(2)}, u32[]{:S(2)}) %collective-permute-start.7) | collective-permute-done | bytes 196640 | tf_op jit(solution)/shard_map/ppermute | solution.py:42
  211.3 1.9 collective-permute-start.8
  213.9 2.1 fusion.15
  215.9 2.6 %collective-permute-done.8 = bf16[2,2,6,2048]{3,0,2,1:T(2,128)(2,1)S(1)} collective-permute-done((bf16[2,2,6,2048]{3,0,2,1:T(2,128)(2,1)S(1)}, bf16[2,2,6,2048]{3,0,2,1:T(2,128)(2,1)S(1)}, u32[]{:S(2)}, u32[]{:S(2)}) %collective-permute-start.8) | collective-permute-done | bytes 98336 | tf_op jit(solution)/shard_map/ppermute | solution.py:42
  218.7 2.9 %collective-permute-start.9 = (bf16[2,6,2048]{2,0,1:T(2,128)(2,1)S(1)}, bf16[2,6,2048]{2,0,1:T(2,128)(2,1)S(1)}, u32[]{:S(2)}, u32[]{:S(2)}) collective-permute-start(bf16[2,6,2048]{2,0,1:T(2,128)(2,1)S(1)} %fusion.20), channel_id=1, source_target_pairs={{0,32},{1,33},{2,34},{3,35},{4,36},{5,37},{6,38},{7,39},{8,40},{9,... | collective-permute-start | bytes 147464 | tf_op jit(solution)/shard_map/ppermute | solution.py:42
  222.6 4.2 %collective-permute-done.9 = bf16[2,6,2048]{2,0,1:T(2,128)(2,1)S(1)} collective-permute-done((bf16[2,6,2048]{2,0,1:T(2,128)(2,1)S(1)}, bf16[2,6,2048]{2,0,1:T(2,128)(2,1)S(1)}, u32[]{:S(2)}, u32[]{:S(2)}) %collective-permute-start.9) | collective-permute-done | bytes 49184 | tf_op jit(solution)/shard_map/ppermute | solution.py:42
  (104 shorter events, 35.1 us)
Async XLA Ops:
  0.6 8.1 %copy-start.8 = (s32[1,1,2]{2,1,0:T(1,128)S(1)}, s32[1,1,2]{2,1,0:T(1,128)}, u32[]{:S(2)}) copy-start(s32[1,1,2]{2,1,0:T(1,128)} %param.34) | copy-start | bytes 28
  0.6 8.7 %copy-start.4 = (bf16[1,6,2048]{2,1,0:T(8,128)(2,1)S(1)}, bf16[1,6,2048]{2,1,0:T(8,128)(2,1)}, u32[]{:S(2)}) copy-start(bf16[1,6,2048]{2,1,0:T(8,128)(2,1)} %param.29) | copy-start | bytes 73732
  0.7 8.7 %copy-start.5 = (bf16[1,6,2048]{2,1,0:T(8,128)(2,1)S(1)}, bf16[1,6,2048]{2,1,0:T(8,128)(2,1)}, u32[]{:S(2)}) copy-start(bf16[1,6,2048]{2,1,0:T(8,128)(2,1)} %param.30) | copy-start | bytes 73732
  4.7 92.8 %collective-permute-start = (bf16[2,128,2048]{2,1,0:T(8,128)(2,1)}, bf16[2,128,2048]{2,1,0:T(8,128)(2,1)}, u32[]{:S(2)}, u32[]{:S(2)}) collective-permute-start(bf16[2,128,2048]{2,1,0:T(8,128)(2,1)} %constant_dynamic-update-slice_fusion), channel_id=1, source_target_pairs={{0,1},{1,2},{2,3},{3,4},{4,5},{5,6},{6,7},{7,8},{8,9},{9,10},{10,1... | collective-permute-start | bytes 3145736 | tf_op jit(solution)/shard_map/ppermute | solution.py:23
  7.4 90.1 %collective-permute-start.1 = (bf16[2,128,2048]{2,1,0:T(8,128)(2,1)}, bf16[2,128,2048]{2,1,0:T(8,128)(2,1)}, u32[]{:S(2)}, u32[]{:S(2)}) collective-permute-start(bf16[2,128,2048]{2,1,0:T(8,128)(2,1)} %constant_dynamic-update-slice_fusion), channel_id=1, source_target_pairs={{1,0},{2,1},{3,2},{4,3},{5,4},{6,5},{7,6},{8,7},{9,8},{10,9},{11,1... | collective-permute-start | bytes 3145736 | tf_op jit(solution)/shard_map/ppermute | solution.py:26
  91.7 5.8 %copy-start.6 = (f32[128]{0:T(128)S(1)}, f32[128]{0:T(128)}, u32[]{:S(2)}) copy-start(f32[128]{0:T(128)} %param.32) | copy-start | bytes 1540
  122.9 1.3 collective-permute-start.10
  124.2 8.9 %collective-permute-start.11 = (f32[2,128]{1,0:T(2,128)S(1)}, f32[2,128]{1,0:T(2,128)S(1)}, u32[]{:S(2)}, u32[]{:S(2)}) collective-permute-start(f32[2,128]{1,0:T(2,128)S(1)} %add.233), channel_id=1, source_target_pairs={{0,2},{1,3},{2,0},{3,1},{4,6},{5,7},{6,4},{7,5},{8,10},{9,11},{10,... | collective-permute-start | bytes 3080 | tf_op jit(solution)/shard_map/ppermute | solution.py:42
  133.1 5.3 %collective-permute-start.12 = (f32[2,128]{1,0:T(2,128)S(1)}, f32[2,128]{1,0:T(2,128)S(1)}, u32[]{:S(2)}, u32[]{:S(2)}) collective-permute-start(f32[2,128]{1,0:T(2,128)S(1)} %add.234), channel_id=1, source_target_pairs={{0,4},{1,5},{2,6},{3,7},{4,0},{5,1},{6,2},{7,3},{8,12},{9,13},{10,... | collective-permute-start | bytes 3080 | tf_op jit(solution)/shard_map/ppermute | solution.py:42
  135.4 23.8 %collective-permute-start.4 = (bf16[2,2,2,2,2,2,6,2048]{7,0,6,5,4,3,2,1:T(2,128)(2,1)S(1)}, bf16[2,2,2,2,2,2,6,2048]{7,0,6,5,4,3,2,1:T(2,128)(2,1)S(1)}, u32[]{:S(2)}, u32[]{:S(2)}) collective-permute-start(bf16[2,2,2,2,2,2,6,2048]{7,0,6,5,4,3,2,1:T(2,128)(2,1)S(1)} %fusion), channel_id=1, source_target_pairs={{0,1},{1,0},{2,3},{3,2},{4,5},{5,4},{6,7},{7,6},{8,9},{9,8},{10,11... | collective-permute-start | bytes 4718600 | tf_op jit(solution)/shard_map/ppermute | solution.py:42
  138.4 4.0 %collective-permute-start.13 = (f32[2,128]{1,0:T(2,128)S(1)}, f32[2,128]{1,0:T(2,128)S(1)}, u32[]{:S(2)}, u32[]{:S(2)}) collective-permute-start(f32[2,128]{1,0:T(2,128)S(1)} %add.235), channel_id=1, source_target_pairs={{0,8},{1,9},{2,10},{3,11},{4,12},{5,13},{6,14},{7,15},{8,0},{9,1},... | collective-permute-start | bytes 3080 | tf_op jit(solution)/shard_map/ppermute | solution.py:42
  142.4 4.5 %collective-permute-start.14 = (f32[2,128]{1,0:T(2,128)S(1)}, f32[2,128]{1,0:T(2,128)S(1)}, u32[]{:S(2)}, u32[]{:S(2)}) collective-permute-start(f32[2,128]{1,0:T(2,128)S(1)} %add.236), channel_id=1, source_target_pairs={{0,16},{1,17},{2,18},{3,19},{4,20},{5,21},{6,22},{7,23},{8,24},{9,... | collective-permute-start | bytes 3080 | tf_op jit(solution)/shard_map/ppermute | solution.py:42
  146.9 7.5 %collective-permute-start.15 = (f32[2,128]{1,0:T(2,128)S(1)}, f32[2,128]{1,0:T(2,128)S(1)}, u32[]{:S(2)}, u32[]{:S(2)}) collective-permute-start(f32[2,128]{1,0:T(2,128)S(1)} %add.237), channel_id=1, source_target_pairs={{0,32},{1,33},{2,34},{3,35},{4,36},{5,37},{6,38},{7,39},{8,40},{9,... | collective-permute-start | bytes 3080 | tf_op jit(solution)/shard_map/ppermute | solution.py:42
  154.4 4.1 %collective-permute-start.16 = (f32[2,128]{1,0:T(2,128)S(1)}, f32[2,128]{1,0:T(2,128)S(1)}, u32[]{:S(2)}, u32[]{:S(2)}) collective-permute-start(f32[2,128]{1,0:T(2,128)S(1)} %add.238), channel_id=1, source_target_pairs={{0,64},{64,0},{128,192},{192,128},{1,65},{65,1},{129,193},{193,129... | collective-permute-start | bytes 3080 | tf_op jit(solution)/shard_map/ppermute | solution.py:42
  155.8 11.8 %collective-permute-start.2 = (bf16[2,128,2048]{2,1,0:T(8,128)(2,1)S(1)}, bf16[2,128,2048]{2,1,0:T(8,128)(2,1)S(1)}, u32[]{:S(2)}, u32[]{:S(2)}) collective-permute-start(bf16[2,128,2048]{2,1,0:T(8,128)(2,1)S(1)} %get-tuple-element.122), channel_id=1, source_target_pairs={{0,1},{1,2},{2,3},{3,4},{4,5},{5,6},{6,7},{7,8},{8,9},{9,10},{10,1... | collective-permute-start | bytes 3145736 | tf_op jit(solution)/shard_map/ppermute | solution.py:23
  157.2 10.4 %collective-permute-start.3 = (bf16[2,128,2048]{2,1,0:T(8,128)(2,1)S(1)}, bf16[2,128,2048]{2,1,0:T(8,128)(2,1)S(1)}, u32[]{:S(2)}, u32[]{:S(2)}) collective-permute-start(bf16[2,128,2048]{2,1,0:T(8,128)(2,1)S(1)} %get-tuple-element.123), channel_id=1, source_target_pairs={{1,0},{2,1},{3,2},{4,3},{5,4},{6,5},{7,6},{8,7},{9,8},{10,9},{11,1... | collective-permute-start | bytes 3145736 | tf_op jit(solution)/shard_map/ppermute | solution.py:26
  158.5 8.6 %collective-permute-start.17 = (f32[2,128]{1,0:T(2,128)S(1)}, f32[2,128]{1,0:T(2,128)S(1)}, u32[]{:S(2)}, u32[]{:S(2)}) collective-permute-start(f32[2,128]{1,0:T(2,128)S(1)} %add.239), channel_id=1, source_target_pairs={{0,128},{64,192},{128,0},{192,64},{1,129},{65,193},{129,1},{193,65... | collective-permute-start | bytes 3080 | tf_op jit(solution)/shard_map/ppermute | solution.py:42
  161.7 31.3 %collective-permute-start.5 = (bf16[2,2,2,2,2,6,2048]{6,0,5,4,3,2,1:T(2,128)(2,1)S(1)}, bf16[2,2,2,2,2,6,2048]{6,0,5,4,3,2,1:T(2,128)(2,1)S(1)}, u32[]{:S(2)}, u32[]{:S(2)}) collective-permute-start(bf16[2,2,2,2,2,6,2048]{6,0,5,4,3,2,1:T(2,128)(2,1)S(1)} %fusion.12), channel_id=1, source_target_pairs={{0,2},{1,3},{2,0},{3,1},{4,6},{5,7},{6,4},{7,5},{8,10},{9,11},{10,... | collective-permute-start | bytes 2359304 | tf_op jit(solution)/shard_map/ppermute | solution.py:42
  168.8 26.7 %copy-start.2 = (f32[16,8,16,128]{3,2,1,0:T(8,128)S(1)}, f32[16,8,16,128]{3,2,1,0:T(8,128)}, u32[]{:S(2)}) copy-start(f32[16,8,16,128]{3,2,1,0:T(8,128)} %copy.26) | copy-start | bytes 3145732
  194.2 9.6 %collective-permute-start.6 = (bf16[2,2,2,2,6,2048]{5,0,4,3,2,1:T(2,128)(2,1)S(1)}, bf16[2,2,2,2,6,2048]{5,0,4,3,2,1:T(2,128)(2,1)S(1)}, u32[]{:S(2)}, u32[]{:S(2)}) collective-permute-start(bf16[2,2,2,2,6,2048]{5,0,4,3,2,1:T(2,128)(2,1)S(1)} %fusion.16), channel_id=1, source_target_pairs={{0,4},{1,5},{2,6},{3,7},{4,0},{5,1},{6,2},{7,3},{8,12},{9,13},{10,... | collective-permute-start | bytes 1179656 | tf_op jit(solution)/shard_map/ppermute | solution.py:42
  196.2 17.7 %copy-start.3 = (bf16[1,128,2048]{2,1,0:T(8,128)(2,1)S(1)}, bf16[1,128,2048]{2,1,0:T(8,128)(2,1)}, u32[]{:S(2)}) copy-start(bf16[1,128,2048]{2,1,0:T(8,128)(2,1)} %param.27) | copy-start | bytes 1572868
  204.6 6.4 %collective-permute-start.7 = (bf16[2,2,2,6,2048]{4,0,3,2,1:T(2,128)(2,1)S(1)}, bf16[2,2,2,6,2048]{4,0,3,2,1:T(2,128)(2,1)S(1)}, u32[]{:S(2)}, u32[]{:S(2)}) collective-permute-start(bf16[2,2,2,6,2048]{4,0,3,2,1:T(2,128)(2,1)S(1)} %fusion.17), channel_id=1, source_target_pairs={{0,8},{1,9},{2,10},{3,11},{4,12},{5,13},{6,14},{7,15},{8,0},{9,1},... | collective-permute-start | bytes 589832 | tf_op jit(solution)/shard_map/ppermute | solution.py:42
  211.3 7.2 %collective-permute-start.8 = (bf16[2,2,6,2048]{3,0,2,1:T(2,128)(2,1)S(1)}, bf16[2,2,6,2048]{3,0,2,1:T(2,128)(2,1)S(1)}, u32[]{:S(2)}, u32[]{:S(2)}) collective-permute-start(bf16[2,2,6,2048]{3,0,2,1:T(2,128)(2,1)S(1)} %fusion.18), channel_id=1, source_target_pairs={{0,16},{1,17},{2,18},{3,19},{4,20},{5,21},{6,22},{7,23},{8,24},{9,... | collective-permute-start | bytes 294920 | tf_op jit(solution)/shard_map/ppermute | solution.py:42
  218.7 8.1 %collective-permute-start.9 = (bf16[2,6,2048]{2,0,1:T(2,128)(2,1)S(1)}, bf16[2,6,2048]{2,0,1:T(2,128)(2,1)S(1)}, u32[]{:S(2)}, u32[]{:S(2)}) collective-permute-start(bf16[2,6,2048]{2,0,1:T(2,128)(2,1)S(1)} %fusion.20), channel_id=1, source_target_pairs={{0,32},{1,33},{2,34},{3,35},{4,36},{5,37},{6,38},{7,39},{8,40},{9,... | collective-permute-start | bytes 147464 | tf_op jit(solution)/shard_map/ppermute | solution.py:42
  (3 other events, 8.6 us)
